TPU v7x, 32 devices: a whole 2x2x4 slice. The times are simulated.
32 devices in a mesh: psg: 8 (over y, x, core), qry: 4 (over z).
Axes of the slice: x: 2, y: 2, z: 4, core: 2. Of those that a mesh axis runs over, the one named last changes fastest.
Arguments:
- hidden: bfloat16 [512, 4096], P('qry'), may hold values from -6 to 6
- norm_gain: float32 [4096], replicated, may hold values from 0.5 to 1.5
- proj_weight: bfloat16 [4096, 4096], P('psg', 'qry'), may hold values from -0.09375 to 0.09375
- pq_codes: int32 [16384, 512], P('psg', 'qry'), may hold values from 0 to 255
- codebook: bfloat16 [512, 8, 256], P('qry'), may hold values from -560 to 560
- positives: int32 [512], replicated, may hold values from 0 to 16383
Outputs:
- losses: float32 [512], P('qry')
- hidden_grad: bfloat16 [512, 4096], P('qry')
- weight_grad: float32 [4096, 4096], P('psg', 'qry')
- codebook_grad: float32 [512, 8, 256], P('qry')
All inputs are finite; a program needn't handle non-finite values.
Results may differ from a plain program's by a relative error of at most 0.019.
The roundings to bfloat16 on the way count: a program that leaves them out, or rounds other values in their place, can miss the bound.
Values may be sent and summed in bfloat16 or wider, within the bound.
No kernel may reach another device: no remote copies, remote signals or barrier semaphores. Data moves between devices by JAX's collectives and lax.ppermute only.
A program may use at most 128 MiB of HBM per device.

v0:
```python
import jax
import jax.numpy as jnp
from jax import lax
from jax.sharding import PartitionSpec as P

score_scale = 0.0625
norm_eps = 1e-06


def code_hot(code_block, book):
    levels = lax.broadcasted_iota(jnp.int32, code_block.shape + (book.shape[2],), 2)
    return (code_block[:, :, None] == levels).astype(jnp.bfloat16)


def per_device(hidden, norm_gain, proj_weight, pq_codes, codebook, positives):
    gathered = lax.all_gather(hidden, "qry", axis=0, tiled=True)
    floats_all = gathered.astype(jnp.float32)
    inverse_all = lax.rsqrt(jnp.mean(floats_all * floats_all, axis=1, keepdims=True) + norm_eps)
    normed = (floats_all * inverse_all * norm_gain[None, :]).astype(jnp.bfloat16)
    columns = proj_weight.shape[1]
    query_float = jnp.dot(
        normed,
        lax.all_gather(proj_weight, "psg", axis=0, tiled=True),
        preferred_element_type=jnp.float32,
    )
    queries = query_float.astype(jnp.bfloat16)
    passage_count = pq_codes.shape[0]
    sub_count = codebook.shape[0]
    sub_width = codebook.shape[1]
    block_rows = min(passage_count, 512)
    code_blocks = pq_codes.reshape(passage_count // block_rows, block_rows, sub_count)

    def decode(code_block):
        hot_table = code_hot(code_block, codebook)
        vectors = jnp.einsum(
            "pmk,mdk->pmd", hot_table, codebook, preferred_element_type=jnp.float32
        )
        return vectors.astype(jnp.bfloat16).reshape(block_rows, columns)

    passages = lax.map(decode, code_blocks).reshape(passage_count, columns)
    partial_value = (
        lax.dot_general(
            queries, passages, (((1,), (1,)), ((), ())), preferred_element_type=jnp.float32
        )
        * score_scale
    )
    qry_index = lax.axis_index("qry")
    own_rows = hidden.shape[0]
    scores = lax.psum_scatter(partial_value, "qry", scatter_dimension=0, tiled=True)
    row_targets = lax.dynamic_slice_in_dim(positives, qry_index * own_rows, own_rows, 0)
    local_target = row_targets - lax.axis_index("psg") * passage_count
    target = lax.broadcasted_iota(jnp.int32, scores.shape, 1) == local_target[:, None]
    local_max = jnp.max(scores, axis=1)
    positive_part = jnp.sum(jnp.where(target, scores, 0.0), axis=1)
    row_max = lax.pmax(local_max, "psg")
    shifted_total = jnp.sum(jnp.exp(scores - row_max[:, None]), axis=1)
    row_total, positive_score = lax.psum((shifted_total, positive_part), "psg")
    losses = jnp.log(row_total) + row_max - positive_score
    score_grad = (
        jnp.exp(scores - row_max[:, None]) / row_total[:, None] - target.astype(jnp.float32)
    ).astype(jnp.bfloat16)
    all_grad = lax.all_gather(score_grad, "qry", axis=0, tiled=True)
    query_part = jnp.dot(all_grad, passages, preferred_element_type=jnp.float32) * score_scale
    query_grad = lax.psum(query_part, "psg").astype(jnp.bfloat16)
    passage_grad = (
        lax.dot_general(
            all_grad, queries, (((0,), (0,)), ((), ())), preferred_element_type=jnp.float32
        )
        * score_scale
    ).astype(jnp.bfloat16)
    grad_blocks = passage_grad.reshape(
        passage_count // block_rows, block_rows, sub_count, sub_width
    )

    def add_book(carry, paired):
        code_block, grad_block = paired
        hot_table = code_hot(code_block, codebook)
        return (
            carry
            + jnp.einsum("pmk,pmd->mdk", hot_table, grad_block, preferred_element_type=jnp.float32),
            None,
        )

    book_part, unused = lax.scan(
        add_book, jnp.zeros(codebook.shape, jnp.float32), (code_blocks, grad_blocks)
    )
    codebook_grad = lax.psum(book_part.astype(jnp.bfloat16), "psg").astype(jnp.float32)
    row_span = proj_weight.shape[0]
    normed_rows = lax.dynamic_slice_in_dim(normed, lax.axis_index("psg") * row_span, row_span, 1)
    weight_grad = lax.dot_general(
        normed_rows, query_grad, (((0,), (0,)), ((), ())), preferred_element_type=jnp.float32
    )
    norm_part = lax.dot_general(
        query_grad,
        lax.all_gather(proj_weight, "psg", axis=0, tiled=True),
        (((1,), (1,)), ((), ())),
        preferred_element_type=jnp.float32,
    )
    norm_back = lax.psum_scatter(
        norm_part.astype(jnp.bfloat16), "qry", scatter_dimension=0, tiled=True
    ).astype(jnp.float32)
    floats_own = hidden.astype(jnp.float32)
    inverse_own = lax.rsqrt(jnp.mean(floats_own * floats_own, axis=1, keepdims=True) + norm_eps)
    scaled = norm_back * norm_gain[None, :]
    hidden_grad = (
        inverse_own * scaled
        - floats_own
        * inverse_own
        * inverse_own
        * inverse_own
        * jnp.mean(scaled * floats_own, axis=1, keepdims=True)
    ).astype(jnp.bfloat16)
    return (losses, hidden_grad, weight_grad, codebook_grad)


def solution(mesh):
    in_specs = (P("qry", None), P(), P("psg", "qry"), P("psg", "qry"), P("qry", None, None), P())
    out_specs = (P("qry"), P("qry", None), P("psg", "qry"), P("qry", None, None))
    return jax.shard_map(
        per_device, mesh=mesh, in_specs=in_specs, out_specs=out_specs, check_vma=False
    )
```

profile of v0, /device:TPU:0, one launch (start us, length us, event | category | flops | bytes accessed | tf_op | source)
XLA Modules:
  0.0 560.6 jit_solution(67081673315906071)
XLA Ops:
  10.3 61.1 %while.21 = (s32[]{:T(128)}, bf16[4,512,1024]{2,1,0:T(8,128)(2,1)}, s32[4,512,128]{1,2,0:T(8,128)S(1)}, bf16[128,8,256]{2,1,0:T(8,128)(2,1)}, s32[]{:T(128)}) while((s32[]{:T(128)}, bf16[4,512,1024]{2,1,0:T(8,128)(2,1)}, s32[4,512,128]{1,2,0:T(8,128)S(1)}, bf16[128,8,256]{2,1,0:T(8,128)(2,1)}, s32[]{:T(128)}) %tuple.45), condition=%wide.region_2.3_spmd, body=%wide.region_1.2_spmd.sunk | while | flops 285736960 | bytes 6553677 | solution.py:40
  10.3 13.6 %fusion.47 = bf16[1,512,1024]{1,2,0:T(8,128)(2,1)S(1)} fusion(bf16[128,8,256]{2,1,0:T(8,128)(2,1)} %get-tuple-element.164, s32[512,128]{0,1:T(8,128)S(1)} %dynamic-slice_bitcast_fusion.4), kind=kOutput, calls=%fused_computation.4.clone.2 | convolution fusion | flops 285736960 | bytes 1835008 | tf_op jit(solution)/shard_map/while/body/eval_jaxpr/pmk,mdk->pmd/dot_general | solution.py:35
  25.7 13.6 %fusion.47 = bf16[1,512,1024]{1,2,0:T(8,128)(2,1)S(1)} fusion(bf16[128,8,256]{2,1,0:T(8,128)(2,1)} %get-tuple-element.164, s32[512,128]{0,1:T(8,128)S(1)} %dynamic-slice_bitcast_fusion.4), kind=kOutput, calls=%fused_computation.4.clone.2 | convolution fusion | flops 285736960 | bytes 1835008 | tf_op jit(solution)/shard_map/while/body/eval_jaxpr/pmk,mdk->pmd/dot_general | solution.py:35
  40.9 13.6 %fusion.47 = bf16[1,512,1024]{1,2,0:T(8,128)(2,1)S(1)} fusion(bf16[128,8,256]{2,1,0:T(8,128)(2,1)} %get-tuple-element.164, s32[512,128]{0,1:T(8,128)S(1)} %dynamic-slice_bitcast_fusion.4), kind=kOutput, calls=%fused_computation.4.clone.2 | convolution fusion | flops 285736960 | bytes 1835008 | tf_op jit(solution)/shard_map/while/body/eval_jaxpr/pmk,mdk->pmd/dot_general | solution.py:35
  56.2 13.6 %fusion.47 = bf16[1,512,1024]{1,2,0:T(8,128)(2,1)S(1)} fusion(bf16[128,8,256]{2,1,0:T(8,128)(2,1)} %get-tuple-element.164, s32[512,128]{0,1:T(8,128)S(1)} %dynamic-slice_bitcast_fusion.4), kind=kOutput, calls=%fused_computation.4.clone.2 | convolution fusion | flops 285736960 | bytes 1835008 | tf_op jit(solution)/shard_map/while/body/eval_jaxpr/pmk,mdk->pmd/dot_general | solution.py:35
  71.4 21.8 %all-gather.4.cloned.1.call-done = bf16[512,4096]{1,0:T(8,128)(2,1)} async-done(((bf16[128,4096]{1,0:T(8,128)(2,1)}), bf16[512,4096]{1,0:T(8,128)(2,1)}) %all-gather.4.cloned.1.call-update) | async-done | bytes 4194320 | tf_op jit(solution)/shard_map/all_gather | solution.py:16
  93.2 3.2 fusion.10
  96.6 3.6 fusion.12
  100.2 47.6 %all-gather.6.cloned.1.call-done = bf16[4096,1024]{1,0:T(8,128)(2,1)} async-done(((bf16[512,1024]{1,0:T(8,128)(2,1)}), bf16[4096,1024]{1,0:T(8,128)(2,1)}) %all-gather.6.cloned.1.call-update) | async-done | bytes 8388624 | tf_op jit(solution)/shard_map/all_gather | solution.py:23
  147.8 9.3 %convolution_convert_fusion.1 = bf16[512,1024]{1,0:T(8,128)(2,1)S(1)} fusion(bf16[512,4096]{1,0:T(8,128)(2,1)} %fusion.12, bf16[4096,1024]{1,0:T(8,128)(2,1)} %all-gather.6.cloned.1.call-done), kind=kOutput, calls=%fused_computation.35 | convolution fusion | flops 4295491584 | bytes 13631488 | tf_op jit(solution)/shard_map/dot_general | solution.py:21
  158.1 4.3 convolution_multiply_fusion
  163.2 76.1 %reduce-scatter.3.cloned.1.call-done = f32[128,2048]{1,0:T(8,128)} async-done(((f32[512,2048]{1,0:T(8,128)}), f32[128,2048]{1,0:T(8,128)}) %reduce-scatter.3.cloned.1.call-update) | async-done | bytes 1048592 | tf_op jit(solution)/shard_map/reduce_scatter | solution.py:49
  240.7 13.3 %pmax.7 = f32[128]{0:T(128)S(1)} all-reduce(f32[128]{0:T(128)S(1)} %reduce_max.9), channel_id=1, replica_groups=mesh['psg'=8,'qry'=4] {'psg'}, use_global_device_ids=true, to_apply=%region_5.6 | all-reduce | flops 128 | bytes 1024 | tf_op jit(solution)/shard_map/pmax | solution.py:55
  255.6 11.8 %psum.28 = f32[128]{0:T(128)S(1)} all-reduce(f32[128]{0:T(128)S(1)} %get-tuple-element.79), channel_id=1, replica_groups=mesh['psg'=8,'qry'=4] {'psg'}, use_global_device_ids=true, to_apply=%region_7.8 | all-reduce | flops 128 | bytes 1024 | tf_op jit(solution)/shard_map/psum | solution.py:57
  267.4 2.4 subtract_convert_fusion
  270.1 44.5 %all-gather.8.cloned.1.call-done = bf16[512,2048]{1,0:T(8,128)(2,1)} async-done(((bf16[128,2048]{1,0:T(8,128)(2,1)}), bf16[512,2048]{1,0:T(8,128)(2,1)}) %all-gather.8.cloned.1.call-update) | async-done | bytes 2097168 | tf_op jit(solution)/shard_map/all_gather | solution.py:62
  314.7 5.3 convolution_multiply_fusion.1
  320.0 4.3 multiply_convert_fusion
  324.3 6.5 %copy.13 = bf16[2048,1024]{0,1:T(8,128)(2,1)} copy(bf16[2048,1024]{1,0:T(8,128)(2,1)} %multiply_convert_fusion) | data formatting | bytes 8388608 | tf_op jit(solution)/shard_map/convert_element_type | solution.py:70
  330.8 7.8 %reshape.49 = bf16[4,512,128,8]{1,0,3,2:T(4,128)(2,1)} reshape(bf16[2048,1024]{0,1:T(8,128)(2,1)} %copy.13) | data formatting | bytes 8388608 | tf_op jit(solution)/shard_map/reshape | solution.py:71
  338.6 5.0 copy.14
  343.6 57.8 %while.22 = (s32[]{:T(128)}, f32[128,8,256]{2,1,0:T(8,128)}, bf16[4,512,128,8]{1,3,2,0:T(8,128)(2,1)}, s32[4,512,128]{1,2,0:T(8,128)S(1)}, s32[]{:T(128)}, /*index=5*/s32[]{:T(128)}) while((s32[]{:T(128)}, f32[128,8,256]{2,1,0:T(8,128)}, bf16[4,512,128,8]{1,3,2,0:T(8,128)(2,1)}, s32[4,512,128]{1,2,0:T(8,128)S(1)}, s32[]{:T(128)}, ...), condition=%wide.region_15.16_spmd.clone, body=%wide.region_14.15_spmd.clone.sunk | while | flops 285736960 | bytes 3932255 | solution.py:84
  343.6 14.4 %fusion.49 = f32[128,8,256]{2,1,0:T(8,128)} fusion(s32[512,128]{0,1:T(8,128)S(1)} %dynamic-slice_bitcast_fusion.5, f32[128,8,256]{2,1,0:T(8,128)} %get-tuple-element.173, bf16[4,512,128,8]{1,3,2,0:T(8,128)(2,1)} %get-tuple-element.180, s32[]{:T(128)S(6)} %copy.31, pred[]{:T(512)S(6)} %compare.3), kind=kOutput, calls=%fused_computation.10.clone.3 | convolution fusion | flops 285736960 | bytes 3407877 | tf_op jit(solution)/shard_map/while/body/eval_jaxpr/pmk,pmd->mdk/dot_general | solution.py:80
  358.1 14.4 %fusion.49 = f32[128,8,256]{2,1,0:T(8,128)} fusion(s32[512,128]{0,1:T(8,128)S(1)} %dynamic-slice_bitcast_fusion.5, f32[128,8,256]{2,1,0:T(8,128)} %get-tuple-element.173, bf16[4,512,128,8]{1,3,2,0:T(8,128)(2,1)} %get-tuple-element.180, s32[]{:T(128)S(6)} %copy.31, pred[]{:T(512)S(6)} %compare.3), kind=kOutput, calls=%fused_computation.10.clone.3 | convolution fusion | flops 285736960 | bytes 3407877 | tf_op jit(solution)/shard_map/while/body/eval_jaxpr/pmk,pmd->mdk/dot_general | solution.py:80
  372.5 14.4 %fusion.49 = f32[128,8,256]{2,1,0:T(8,128)} fusion(s32[512,128]{0,1:T(8,128)S(1)} %dynamic-slice_bitcast_fusion.5, f32[128,8,256]{2,1,0:T(8,128)} %get-tuple-element.173, bf16[4,512,128,8]{1,3,2,0:T(8,128)(2,1)} %get-tuple-element.180, s32[]{:T(128)S(6)} %copy.31, pred[]{:T(512)S(6)} %compare.3), kind=kOutput, calls=%fused_computation.10.clone.3 | convolution fusion | flops 285736960 | bytes 3407877 | tf_op jit(solution)/shard_map/while/body/eval_jaxpr/pmk,pmd->mdk/dot_general | solution.py:80
  387.0 14.4 %fusion.49 = f32[128,8,256]{2,1,0:T(8,128)} fusion(s32[512,128]{0,1:T(8,128)S(1)} %dynamic-slice_bitcast_fusion.5, f32[128,8,256]{2,1,0:T(8,128)} %get-tuple-element.173, bf16[4,512,128,8]{1,3,2,0:T(8,128)(2,1)} %get-tuple-element.180, s32[]{:T(128)S(6)} %copy.31, pred[]{:T(512)S(6)} %compare.3), kind=kOutput, calls=%fused_computation.10.clone.3 | convolution fusion | flops 285736960 | bytes 3407877 | tf_op jit(solution)/shard_map/while/body/eval_jaxpr/pmk,pmd->mdk/dot_general | solution.py:80
  403.6 60.3 %all-reduce.5 = (f32[128]{0:T(128)S(1)}, bf16[512,1024]{1,0:T(8,128)(2,1)S(1)}) all-reduce(f32[128]{0:T(128)S(1)} %get-tuple-element.80, f32[512,1024]{1,0:T(8,128)S(1)} %convolution_multiply_fusion.1), channel_id=1, replica_groups=mesh['psg'=8,'qry'=4] {'psg'}, use_global_device_ids=true, to_apply=%region_9.10 | all-reduce | flops 524416 | bytes 3146752 | tf_op jit(solution)/shard_map/psum | solution.py:57
  463.9 9.9 %convolution_convert_fusion = bf16[512,4096]{1,0:T(8,128)(2,1)} fusion(bf16[4096,1024]{1,0:T(8,128)(2,1)} %all-gather.6.cloned.1.call-done, bf16[512,1024]{1,0:T(8,128)(2,1)S(1)} %get-tuple-element.98), kind=kOutput, calls=%fused_computation.21 | convolution fusion | flops 4297064448 | bytes 13631488 | tf_op jit(solution)/shard_map/dot_general | solution.py:93
  475.0 3.1 fusion.21
  478.1 2.2 convert_element_type.59
  480.3 68.7 %reduce-scatter.5.cloned.1.call-done = bf16[128,4096]{1,0:T(8,128)(2,1)} async-done(((bf16[512,4096]{1,0:T(8,128)(2,1)}), bf16[128,4096]{1,0:T(8,128)(2,1)}) %reduce-scatter.5.cloned.1.call-update) | async-done | bytes 1048592 | tf_op jit(solution)/shard_map/reduce_scatter | solution.py:99
  550.8 2.9 fusion.18
  (58 shorter events, 20.0 us)
Async XLA Ops:
  7.2 86.0 %all-gather.4.cloned.1.call-start = ((), (), s32[]{:S(2)}) async-start(), calls=%async_computation.2 | async-start | bytes 5242880 | tf_op jit(solution)/shard_map/all_gather | solution.py:16
  7.9 139.9 %all-gather.6.cloned.1.call-start = ((), (), s32[]{:S(2)}) async-start(), calls=%async_computation.3 | async-start | bytes 9437184 | tf_op jit(solution)/shard_map/all_gather | solution.py:23
  8.6 230.7 %reduce-scatter.3.cloned.1.call-start = ((), (), s32[]{:S(2)}) async-start(), calls=%async_computation.4 | async-start | bytes 5242880 | tf_op jit(solution)/shard_map/reduce_scatter | solution.py:49
  10.3 86.2 %copy-start.4 = (f32[4096]{0:T(1024)S(1)}, f32[4096]{0:T(1024)}, u32[]{:S(2)}) copy-start(f32[4096]{0:T(1024)} %param.11) | copy-start | bytes 49156
  93.2 3.4 copy-start
  147.8 10.3 %copy-start.5 = (bf16[4,512,1024]{2,1,0:T(8,128)(2,1)S(1)}, bf16[4,512,1024]{2,1,0:T(8,128)(2,1)}, u32[]{:S(2)}) copy-start(bf16[4,512,1024]{2,1,0:T(8,128)(2,1)} %get-tuple-element.48) | copy-start | bytes 12582916
  157.1 1.0 copy-start.7
  162.4 152.3 %all-gather.8.cloned.1.call-start = ((), (), s32[]{:S(2)}) async-start(), calls=%async_computation.5 | async-start | bytes 2621440 | tf_op jit(solution)/shard_map/all_gather | solution.py:62
  269.9 208.2 %all-reduce.4.cloned.1.call-start = ((), (), s32[]{:S(2)}) async-start(), calls=%async_computation.7 | async-start | bytes 1048576 | tf_op jit(solution)/shard_map/psum | solution.py:87
  314.7 5.3 copy-start.6
  314.7 5.3 copy-start.8
  403.5 145.5 %reduce-scatter.5.cloned.1.call-start = ((), (), s32[]{:S(2)}) async-start(), calls=%async_computation.6 | async-start | bytes 5242880 | tf_op jit(solution)/shard_map/reduce_scatter | solution.py:99
  463.9 9.9 %copy-start.2 = (bf16[512,1024]{1,0:T(8,128)(2,1)}, bf16[512,1024]{1,0:T(8,128)(2,1)S(1)}, u32[]{:S(2)}) copy-start(bf16[512,1024]{1,0:T(8,128)(2,1)S(1)} %get-tuple-element.98) | copy-start | bytes 3145732
  473.8 1.2 copy-start.3
  473.8 75.2 %copy-start.1 = (bf16[128,4096]{1,0:T(8,128)(2,1)S(1)}, bf16[128,4096]{1,0:T(8,128)(2,1)}, u32[]{:S(2)}) copy-start(bf16[128,4096]{1,0:T(8,128)(2,1)} %param.10) | copy-start | bytes 3145732
Sparse Core Ops, SparseCore 0:
  9.5 83.5 all-gather.3
  95.1 52.7 all-gather.5
  162.5 76.7 reduce-scatter.2
  270.0 44.5 all-gather.7
  403.7 54.7 all-reduce.3
  473.9 75.0 reduce-scatter.4
where the time goes:
time: 562 us; the launch traced here: 561 us
  waiting for transfers between devices  260 us (46%)
  matrix products  148 us (26%)
  blocking collectives  85.4 us (15%)
  local copies, waits for them, and re-layouts  29.3 us (5%)
  other arithmetic  22.6 us (4%)
  between operations  14.2 us (3%)
    reduce_scatter x1, waiting for transfers between devices, per_device(): lax.psum_scatter(partial_value, 'qry', scatter_dimension=0, tiled=True)  76.1 us
    psum x2, blocking collectives, per_device(): row_total, positive_score = lax.psum((shifted_total, positive_part), 'psg')  72.1 us
    reduce_scatter x1, waiting for transfers between devices, per_device(): lax.psum_scatter(norm_part.astype(jnp.bfloat16), 'qry', scatter_dimension...  68.7 us
    dot_general x4, matrix products, add_book(): jnp.einsum('pmk,pmd->mdk', hot_table, grad_block, preferred_element_type=...  57.7 us
    dot_general x4, matrix products, decode(): jnp.einsum('pmk,mdk->pmd', hot_table, codebook, preferred_element_type=jn...  54.6 us
    all_gather x1, waiting for transfers between devices, per_device(): lax.all_gather(proj_weight, 'psg', axis=0, tiled=True)  47.6 us
    all_gather x1, waiting for transfers between devices, per_device(): all_grad = lax.all_gather(score_grad, 'qry', axis=0, tiled=True)  44.5 us
    all_gather x1, waiting for transfers between devices, per_device(): gathered = lax.all_gather(hidden, 'qry', axis=0, tiled=True)  21.8 us
  transfers between devices with their start and end apart: 6, of which 5 were waited for; matrix products, arithmetic and copies ran while one was open for 15% of the time, Pallas kernels for 0%

commit v1 on v0

--- a/solution.py
+++ b/solution.py
@@ -5,6 +5,12 @@
 
 score_scale = 0.0625
 norm_eps = 1e-06
+
+
+def group_resolve(local_values, d0):
+    finding = jnp.stack([local_values for _ in range(lax.axis_size("psg"))], 0)
+    frame_out = lax.all_to_all(finding, "psg", 0, 0)
+    return jnp.concatenate(frame_out, d0)
 
 
 def code_hot(code_block, book):
@@ -18,11 +24,7 @@
     inverse_all = lax.rsqrt(jnp.mean(floats_all * floats_all, axis=1, keepdims=True) + norm_eps)
     normed = (floats_all * inverse_all * norm_gain[None, :]).astype(jnp.bfloat16)
     columns = proj_weight.shape[1]
-    query_float = jnp.dot(
-        normed,
-        lax.all_gather(proj_weight, "psg", axis=0, tiled=True),
-        preferred_element_type=jnp.float32,
-    )
+    query_float = jnp.dot(normed, group_resolve(proj_weight, 0), preferred_element_type=jnp.float32)
     queries = query_float.astype(jnp.bfloat16)
     passage_count = pq_codes.shape[0]
     sub_count = codebook.shape[0]

time: 562 us -> 581 us (1.034)
  matrix products: 148 us -> 158 us
    all_gather x1, waiting for transfers between devices: 47.6 us -> 0.02 us  [per_device(): lax.all_gather(proj_weight, 'psg', axis=0, tiled=True)]
    psum x1, waiting for transfers between devices: 0.01 us -> 40.1 us  [per_device(): lax.psum(book_part.astype(jnp.bfloat16), 'psg').astype(jnp.float32)]
    all_to_all x0 -> x1, waiting for transfers between devices: none -> 13.2 us  [group_resolve(): frame_out = lax.all_to_all(finding, 'psg', 0, 0)]
    all_gather x1, waiting for transfers between devices: 21.8 us -> 12.8 us  [per_device(): gathered = lax.all_gather(hidden, 'qry', axis=0, tiled=True)]
    dot_general x4, matrix products: 57.7 us -> 66.6 us  [add_book(): jnp.einsum('pmk,pmd->mdk', hot_table, grad_block, preferred_element_type=...]
    reduce_scatter x1, waiting for transfers between devices: 68.7 us -> 76.2 us  [per_device(): lax.psum_scatter(norm_part.astype(jnp.bfloat16), 'qry', scatter_dimension...]
  transfers between devices with their start and end apart: 6 -> 7, of which waited for: 5 -> 6; matrix products, arithmetic and copies ran while one was open for 15% -> 32% of each run, Pallas kernels for 0% -> 0%
where the time goes in v1:
time: 581 us; the launch traced here: 579 us
  waiting for transfers between devices  264 us (45%)
  matrix products  158 us (27%)
  blocking collectives  83 us (14%)
  local copies, waits for them, and re-layouts  33 us (6%)
  other arithmetic  21.1 us (4%)
  between operations  14.2 us (2%)
    reduce_scatter x1, waiting for transfers between devices, per_device(): lax.psum_scatter(partial_value, 'qry', scatter_dimension=0, tiled=True)  76.3 us
    reduce_scatter x1, waiting for transfers between devices, per_device(): lax.psum_scatter(norm_part.astype(jnp.bfloat16), 'qry', scatter_dimension...  76.2 us
    psum x2, blocking collectives, per_device(): row_total, positive_score = lax.psum((shifted_total, positive_part), 'psg')  69.7 us
    dot_general x4, matrix products, add_book(): jnp.einsum('pmk,pmd->mdk', hot_table, grad_block, preferred_element_type=...  66.6 us
    dot_general x4, matrix products, decode(): jnp.einsum('pmk,mdk->pmd', hot_table, codebook, preferred_element_type=jn...  54.6 us
    all_gather x1, waiting for transfers between devices, per_device(): all_grad = lax.all_gather(score_grad, 'qry', axis=0, tiled=True)  44 us
    psum x1, waiting for transfers between devices, per_device(): lax.psum(book_part.astype(jnp.bfloat16), 'psg').astype(jnp.float32)  40.1 us
    pmax x1, blocking collectives, per_device(): row_max = lax.pmax(local_max, 'psg')  13.3 us
  transfers between devices with their start and end apart: 7, of which 6 were waited for; matrix products, arithmetic and copies ran while one was open for 32% of the time, Pallas kernels for 0%

profile of v1, /device:TPU:0, one launch (start us, length us, event | category | flops | bytes accessed | tf_op | source)
XLA Modules:
  0.0 579.4 jit_solution(10775751643776645967)
XLA Ops:
  7.9 5.5 stack.2
  13.4 5.3 all-to-all-start
  19.2 61.1 %while.21 = (s32[]{:T(128)}, bf16[4,512,1024]{2,1,0:T(8,128)(2,1)}, s32[4,512,128]{1,2,0:T(8,128)S(1)}, bf16[128,8,256]{2,1,0:T(8,128)(2,1)}, s32[]{:T(128)}) while((s32[]{:T(128)}, bf16[4,512,1024]{2,1,0:T(8,128)(2,1)}, s32[4,512,128]{1,2,0:T(8,128)S(1)}, bf16[128,8,256]{2,1,0:T(8,128)(2,1)}, s32[]{:T(128)}) %tuple.45), condition=%wide.region_2.3_spmd, body=%wide.region_1.2_spmd.sunk | while | flops 285736960 | bytes 6554177 | solution.py:42
  19.2 13.6 %fusion.47 = bf16[1,512,1024]{1,2,0:T(8,128)(2,1)S(1)} fusion(bf16[128,8,256]{2,1,0:T(8,128)(2,1)} %get-tuple-element.164, s32[512,128]{0,1:T(8,128)S(1)} %dynamic-slice_bitcast_fusion.4), kind=kOutput, calls=%fused_computation.4.clone.2 | convolution fusion | flops 285736960 | bytes 1835008 | tf_op jit(solution)/shard_map/while/body/eval_jaxpr/pmk,mdk->pmd/dot_general | solution.py:37
  34.5 13.6 %fusion.47 = bf16[1,512,1024]{1,2,0:T(8,128)(2,1)S(1)} fusion(bf16[128,8,256]{2,1,0:T(8,128)(2,1)} %get-tuple-element.164, s32[512,128]{0,1:T(8,128)S(1)} %dynamic-slice_bitcast_fusion.4), kind=kOutput, calls=%fused_computation.4.clone.2 | convolution fusion | flops 285736960 | bytes 1835008 | tf_op jit(solution)/shard_map/while/body/eval_jaxpr/pmk,mdk->pmd/dot_general | solution.py:37
  49.8 13.6 %fusion.47 = bf16[1,512,1024]{1,2,0:T(8,128)(2,1)S(1)} fusion(bf16[128,8,256]{2,1,0:T(8,128)(2,1)} %get-tuple-element.164, s32[512,128]{0,1:T(8,128)S(1)} %dynamic-slice_bitcast_fusion.4), kind=kOutput, calls=%fused_computation.4.clone.2 | convolution fusion | flops 285736960 | bytes 1835008 | tf_op jit(solution)/shard_map/while/body/eval_jaxpr/pmk,mdk->pmd/dot_general | solution.py:37
  65.0 13.6 %fusion.47 = bf16[1,512,1024]{1,2,0:T(8,128)(2,1)S(1)} fusion(bf16[128,8,256]{2,1,0:T(8,128)(2,1)} %get-tuple-element.164, s32[512,128]{0,1:T(8,128)S(1)} %dynamic-slice_bitcast_fusion.4), kind=kOutput, calls=%fused_computation.4.clone.2 | convolution fusion | flops 285736960 | bytes 1835008 | tf_op jit(solution)/shard_map/while/body/eval_jaxpr/pmk,mdk->pmd/dot_general | solution.py:37
  80.3 12.8 %all-gather.4.cloned.1.call-done = bf16[512,4096]{1,0:T(8,128)(2,1)} async-done(((bf16[128,4096]{1,0:T(8,128)(2,1)}), bf16[512,4096]{1,0:T(8,128)(2,1)}) %all-gather.4.cloned.1.call-update) | async-done | bytes 4194320 | tf_op jit(solution)/shard_map/all_gather | solution.py:22
  93.0 3.2 fusion.10
  96.5 3.5 fusion.12
  100.0 13.2 %all-to-all-done = bf16[8,512,1024]{2,1,0:T(8,128)(2,1)} async-done(((bf16[8,512,1024]{2,1,0:T(8,128)(2,1)}), bf16[8,512,1024]{2,1,0:T(8,128)(2,1)}, u32[]{:S(2)}, u32[]{:S(2)}) %all-to-all-start) | async-done | bytes 8388640 | tf_op jit(solution)/shard_map/all_to_all | solution.py:12
  113.3 9.3 %convolution_convert_fusion.1 = bf16[512,1024]{1,0:T(8,128)(2,1)S(1)} fusion(bf16[512,4096]{1,0:T(8,128)(2,1)} %fusion.12, bf16[4096,1024]{1,0:T(8,128)(2,1)} %bitcast.3), kind=kOutput, calls=%fused_computation.35 | convolution fusion | flops 4295491584 | bytes 13631488 | tf_op jit(solution)/shard_map/dot_general | solution.py:27
  123.5 4.3 convolution_multiply_fusion
  128.7 76.3 %reduce-scatter.3.cloned.1.call-done = f32[128,2048]{1,0:T(8,128)} async-done(((f32[512,2048]{1,0:T(8,128)}), f32[128,2048]{1,0:T(8,128)}) %reduce-scatter.3.cloned.1.call-update) | async-done | bytes 1048592 | tf_op jit(solution)/shard_map/reduce_scatter | solution.py:51
  206.3 13.3 %pmax.7 = f32[128]{0:T(128)S(1)} all-reduce(f32[128]{0:T(128)S(1)} %reduce_max.9), channel_id=1, replica_groups=mesh['psg'=8,'qry'=4] {'psg'}, use_global_device_ids=true, to_apply=%region_5.6 | all-reduce | flops 128 | bytes 1024 | tf_op jit(solution)/shard_map/pmax | solution.py:57
  221.2 11.8 %psum.28 = f32[128]{0:T(128)S(1)} all-reduce(f32[128]{0:T(128)S(1)} %get-tuple-element.79), channel_id=1, replica_groups=mesh['psg'=8,'qry'=4] {'psg'}, use_global_device_ids=true, to_apply=%region_7.8 | all-reduce | flops 128 | bytes 1024 | tf_op jit(solution)/shard_map/psum | solution.py:59
  236.3 44.0 %all-gather.6.cloned.1.call-done = bf16[512,2048]{1,0:T(8,128)(2,1)} async-done(((bf16[128,2048]{1,0:T(8,128)(2,1)}), bf16[512,2048]{1,0:T(8,128)(2,1)}) %all-gather.6.cloned.1.call-update) | async-done | bytes 2097168 | tf_op jit(solution)/shard_map/all_gather | solution.py:64
  280.3 6.6 %convolution_multiply_fusion.1 = f32[512,1024]{1,0:T(8,128)} fusion(bf16[512,2048]{1,0:T(8,128)(2,1)} %all-gather.6.cloned.1.call-done, bf16[2048,1024]{1,0:T(8,128)(2,1)} %bitcast.44), kind=kOutput, calls=%fused_computation.34 | convolution fusion | flops 2148007936 | bytes 8388608 | tf_op jit(solution)/shard_map/dot_general | solution.py:65
  286.9 4.3 multiply_convert_fusion
  291.3 6.5 %copy.13 = bf16[2048,1024]{0,1:T(8,128)(2,1)} copy(bf16[2048,1024]{1,0:T(8,128)(2,1)} %multiply_convert_fusion) | data formatting | bytes 8388608 | tf_op jit(solution)/shard_map/convert_element_type | solution.py:72
  297.7 7.8 %reshape.55 = bf16[4,512,128,8]{1,0,3,2:T(4,128)(2,1)} reshape(bf16[2048,1024]{0,1:T(8,128)(2,1)} %copy.13) | data formatting | bytes 8388608 | tf_op jit(solution)/shard_map/reshape | solution.py:73
  305.6 5.0 copy.14
  310.6 66.8 %while.22 = (s32[]{:T(128)}, f32[128,8,256]{2,1,0:T(8,128)S(1)}, bf16[4,512,128,8]{1,3,2,0:T(8,128)(2,1)}, s32[4,512,128]{1,2,0:T(8,128)S(1)}, s32[]{:T(128)}, /*index=5*/s32[]{:T(128)}) while((s32[]{:T(128)}, f32[128,8,256]{2,1,0:T(8,128)S(1)}, bf16[4,512,128,8]{1,3,2,0:T(8,128)(2,1)}, s32[4,512,128]{1,2,0:T(8,128)S(1)}, ...), condition=%wide.region_15.16_spmd.clone, body=%wide.region_14.15_spmd.clone.sunk | while | flops 285736960 | bytes 3932755 | solution.py:86
  310.6 16.7 %fusion.49 = f32[128,8,256]{2,1,0:T(8,128)S(1)} fusion(s32[512,128]{0,1:T(8,128)S(1)} %dynamic-slice_bitcast_fusion.5, f32[128,8,256]{2,1,0:T(8,128)S(1)} %get-tuple-element.173, bf16[4,512,128,8]{1,3,2,0:T(8,128)(2,1)} %get-tuple-element.180, s32[]{:T(128)} %get-tuple-element.172, pred[]{:T(512)S(6)} %compare.3), kind=kOutput, calls=%fused_computation.10.clone.3 | convolution fusion | flops 285736960 | bytes 3408385 | tf_op jit(solution)/shard_map/while/body/eval_jaxpr/pmk,pmd->mdk/dot_general | solution.py:82
  327.3 16.7 %fusion.49 = f32[128,8,256]{2,1,0:T(8,128)S(1)} fusion(s32[512,128]{0,1:T(8,128)S(1)} %dynamic-slice_bitcast_fusion.5, f32[128,8,256]{2,1,0:T(8,128)S(1)} %get-tuple-element.173, bf16[4,512,128,8]{1,3,2,0:T(8,128)(2,1)} %get-tuple-element.180, s32[]{:T(128)} %get-tuple-element.172, pred[]{:T(512)S(6)} %compare.3), kind=kOutput, calls=%fused_computation.10.clone.3 | convolution fusion | flops 285736960 | bytes 3408385 | tf_op jit(solution)/shard_map/while/body/eval_jaxpr/pmk,pmd->mdk/dot_general | solution.py:82
  344.1 16.7 %fusion.49 = f32[128,8,256]{2,1,0:T(8,128)S(1)} fusion(s32[512,128]{0,1:T(8,128)S(1)} %dynamic-slice_bitcast_fusion.5, f32[128,8,256]{2,1,0:T(8,128)S(1)} %get-tuple-element.173, bf16[4,512,128,8]{1,3,2,0:T(8,128)(2,1)} %get-tuple-element.180, s32[]{:T(128)} %get-tuple-element.172, pred[]{:T(512)S(6)} %compare.3), kind=kOutput, calls=%fused_computation.10.clone.3 | convolution fusion | flops 285736960 | bytes 3408385 | tf_op jit(solution)/shard_map/while/body/eval_jaxpr/pmk,pmd->mdk/dot_general | solution.py:82
  360.8 16.7 %fusion.49 = f32[128,8,256]{2,1,0:T(8,128)S(1)} fusion(s32[512,128]{0,1:T(8,128)S(1)} %dynamic-slice_bitcast_fusion.5, f32[128,8,256]{2,1,0:T(8,128)S(1)} %get-tuple-element.173, bf16[4,512,128,8]{1,3,2,0:T(8,128)(2,1)} %get-tuple-element.180, s32[]{:T(128)} %get-tuple-element.172, pred[]{:T(512)S(6)} %compare.3), kind=kOutput, calls=%fused_computation.10.clone.3 | convolution fusion | flops 285736960 | bytes 3408385 | tf_op jit(solution)/shard_map/while/body/eval_jaxpr/pmk,pmd->mdk/dot_general | solution.py:82
  378.3 57.9 %all-reduce.5 = (f32[128]{0:T(128)S(1)}, bf16[512,1024]{1,0:T(8,128)(2,1)S(1)}) all-reduce(f32[128]{0:T(128)S(1)} %get-tuple-element.80, f32[512,1024]{1,0:T(8,128)} %convolution_multiply_fusion.1), channel_id=1, replica_groups=mesh['psg'=8,'qry'=4] {'psg'}, use_global_device_ids=true, to_apply=%region_9.10 | all-reduce | flops 524416 | bytes 3146752 | tf_op jit(solution)/shard_map/psum | solution.py:59
  436.3 9.4 %convolution_convert_fusion = bf16[512,4096]{1,0:T(8,128)(2,1)} fusion(bf16[4096,1024]{1,0:T(8,128)(2,1)} %all-gather.8.cloned.1.call-done, bf16[512,1024]{1,0:T(8,128)(2,1)S(1)} %get-tuple-element.98), kind=kOutput, calls=%fused_computation.21 | convolution fusion | flops 4297064448 | bytes 13631488 | tf_op jit(solution)/shard_map/dot_general | solution.py:95
  446.3 3.1 fusion.21
  449.4 40.1 %all-reduce.4.cloned.1.call-done = bf16[128,8,256]{2,1,0:T(8,128)(2,1)} async-done(((bf16[128,8,256]{2,1,0:T(8,128)(2,1)}), bf16[128,8,256]{2,1,0:T(8,128)(2,1)}) %all-reduce.4.cloned.1.call-update) | async-done | bytes 524304 | tf_op jit(solution)/shard_map/psum | solution.py:89
  491.6 76.2 %reduce-scatter.5.cloned.1.call-done = bf16[128,4096]{1,0:T(8,128)(2,1)} async-done(((bf16[512,4096]{1,0:T(8,128)(2,1)}), bf16[128,4096]{1,0:T(8,128)(2,1)}) %reduce-scatter.5.cloned.1.call-update) | async-done | bytes 1048592 | tf_op jit(solution)/shard_map/reduce_scatter | solution.py:101
  (59 shorter events, 24.2 us)
Async XLA Ops:
  7.2 85.9 %all-gather.4.cloned.1.call-start = ((), (), s32[]{:S(2)}) async-start(), calls=%async_computation.3 | async-start | bytes 5242880 | tf_op jit(solution)/shard_map/all_gather | solution.py:22
  13.4 5.4 copy-start.2
  13.4 99.8 %all-to-all-start = ((bf16[8,512,1024]{2,1,0:T(8,128)(2,1)}), bf16[8,512,1024]{2,1,0:T(8,128)(2,1)}, u32[]{:S(2)}, u32[]{:S(2)}) async-start(bf16[8,512,1024]{2,1,0:T(8,128)(2,1)} %stack.2), calls=%async_computation | async-start | bytes 16777216 | tf_op jit(solution)/shard_map/all_to_all | solution.py:12
  18.8 186.2 %reduce-scatter.3.cloned.1.call-start = ((), (), s32[]{:S(2)}) async-start(), calls=%async_computation.4 | async-start | bytes 5242880 | tf_op jit(solution)/shard_map/reduce_scatter | solution.py:51
  19.2 77.1 %copy-start.3 = (f32[4096]{0:T(1024)S(1)}, f32[4096]{0:T(1024)}, u32[]{:S(2)}) copy-start(f32[4096]{0:T(1024)} %param.11) | copy-start | bytes 49156
  93.0 3.4 copy-start
  113.3 10.3 %copy-start.4 = (bf16[4,512,1024]{2,1,0:T(8,128)(2,1)S(1)}, bf16[4,512,1024]{2,1,0:T(8,128)(2,1)}, u32[]{:S(2)}) copy-start(bf16[4,512,1024]{2,1,0:T(8,128)(2,1)} %get-tuple-element.48) | copy-start | bytes 12582916
  122.5 1.0 copy-start.6
  127.8 152.4 %all-gather.6.cloned.1.call-start = ((), (), s32[]{:S(2)}) async-start(), calls=%async_computation.5 | async-start | bytes 2621440 | tf_op jit(solution)/shard_map/all_gather | solution.py:64
  235.5 200.8 %all-gather.8.cloned.1.call-start = ((), (), s32[]{:S(2)}) async-start(), calls=%async_computation.6 | async-start | bytes 9437184 | tf_op jit(solution)/shard_map/all_gather | solution.py:97
  236.1 253.5 %all-reduce.4.cloned.1.call-start = ((), (), s32[]{:S(2)}) async-start(), calls=%async_computation.8 | async-start | bytes 1048576 | tf_op jit(solution)/shard_map/psum | solution.py:89
  280.3 6.6 %copy-start.5 = (bf16[512,2048]{1,0:T(8,128)(2,1)S(1)}, bf16[512,2048]{1,0:T(8,128)(2,1)}, u32[]{:S(2)}) copy-start(bf16[512,2048]{1,0:T(8,128)(2,1)} %all-gather.6.cloned.1.call-done) | copy-start | bytes 6291460
  280.3 6.6 %copy-start.7 = (bf16[512,1024]{1,0:T(8,128)(2,1)S(1)}, bf16[512,1024]{1,0:T(8,128)(2,1)}, u32[]{:S(2)}) copy-start(bf16[512,1024]{1,0:T(8,128)(2,1)} %copy-done.6) | copy-start | bytes 3145732
  436.2 131.6 %reduce-scatter.5.cloned.1.call-start = ((), (), s32[]{:S(2)}) async-start(), calls=%async_computation.7 | async-start | bytes 5242880 | tf_op jit(solution)/shard_map/reduce_scatter | solution.py:101
  445.8 122.0 %copy-start.1 = (bf16[128,4096]{1,0:T(8,128)(2,1)S(1)}, bf16[128,4096]{1,0:T(8,128)(2,1)}, u32[]{:S(2)}) copy-start(bf16[128,4096]{1,0:T(8,128)(2,1)} %param.10) | copy-start | bytes 3145732
Sparse Core Ops, SparseCore 0:
  9.5 83.4 all-gather.3
  128.0 76.9 reduce-scatter.2
  235.6 44.6 all-gather.5
  282.0 53.1 all-gather.7
  436.4 53.1 all-reduce.3
  491.7 76.0 reduce-scatter.4
